TPU v7x, 256 devices: a whole 4x4x8 slice. The times are simulated.
256 devices in a mesh: seq: 32 (over z, x), fsdp: 8 (over y, core).
Axes of the slice: x: 4, y: 4, z: 8, core: 2. Of those that a mesh axis runs over, the one named last changes fastest.
Arguments:
- tokens: bfloat16 [24576, 6144], P('seq'), may hold values from -30 to 30
- w_query: bfloat16 [6144, 32, 128], P('seq', 'fsdp'), may hold values from -0.078125 to 0.078125
- w_keyval: bfloat16 [6144, 32, 256], P('seq', 'fsdp'), may hold values from -40 to 40
- doc_lengths: int32 [8], replicated, may hold values from 1 to 12288, 24576 in all
- norm_gain: bfloat16 [4096], P('fsdp'), may hold values from 0.25 to 1.75
Outputs:
- attended: bfloat16 [24576, 4096], P('seq', 'fsdp')
Inputs may be any that keep to these rules, and one draw needn't show every extreme that they name: `doc_lengths`: lengths are positive and sum to 24576; the longest document has exactly 12288 tokens.
All inputs are finite; a program needn't handle non-finite values.
Results may differ from a plain program's by a relative error of at most 0.0034.
Values may be sent and summed in bfloat16 or wider, within the bound.
A program may use at most 128 MiB of HBM per device.

v0:
```python
import jax
import jax.numpy as jnp
from jax import lax
from jax.sharding import PartitionSpec as P


def carried_in(value, axis, join, neutral):
    count, mine = (lax.axis_size(axis), lax.axis_index(axis))
    pieces = jax.tree.map(lambda part: lax.all_gather(part, axis), value)
    running = jax.tree.map(
        lambda part, zero: jnp.full_like(part, 0) + jnp.asarray(zero, part.dtype), value, neutral
    )

    def step(position, running):
        longer = join(running, jax.tree.map(lambda part: part[position], pieces))
        return jax.tree.map(lambda new, old: jnp.where(position < mine, new, old), longer, running)

    return lax.fori_loop(0, count - 1, step, running)


def doc_index(positions, doc_ends):
    return jnp.sum((positions[:, None] >= doc_ends[None, :]).astype(jnp.int32), axis=1)


def shards(tokens, w_query, w_keyval, doc_lengths, norm_gain):
    rows_here = tokens.shape[0]
    head_count = w_query.shape[1]
    head_size = w_query.shape[2]
    shard_index = lax.axis_index("seq")
    doc_ends = jnp.cumsum(doc_lengths)
    offsets = lax.iota(jnp.int32, rows_here)
    doc_ids = doc_index(shard_index * rows_here + offsets, doc_ends)
    first_doc = doc_ids[0]
    tail_doc = doc_ids[rows_here - 1]

    def project(panel_rows):
        panel = panel_rows.reshape(panel_rows.shape[0], panel_rows.shape[1] * panel_rows.shape[2])
        return jnp.dot(tokens, panel, preferred_element_type=jnp.float32)

    query_sum = project(lax.all_gather(w_query, "seq", axis=0, tiled=True))
    keyval_sum = project(lax.all_gather(w_keyval, "seq", axis=0, tiled=True))
    keyval = (
        jax.nn.silu(keyval_sum).astype(jnp.bfloat16).reshape(rows_here, head_count, 2 * head_size)
    )
    key_rows = keyval[:, :, :head_size]
    values = keyval[:, :, head_size:]
    tail_mask = (doc_ids == tail_doc).astype(jnp.bfloat16)
    tail_state = jnp.einsum(
        "thd,the->hde",
        key_rows * tail_mask[:, None, None],
        values,
        preferred_element_type=jnp.float32,
    )
    tail_begin = doc_ends[tail_doc] - doc_lengths[tail_doc]
    restart = (tail_begin >= shard_index * rows_here).astype(jnp.float32)

    def combine(earlier, newer):
        return (newer[0] + (1.0 - newer[1]) * earlier[0], jnp.maximum(earlier[1], newer[1]))

    incoming, _ = carried_in(
        (tail_state, restart),
        "seq",
        combine,
        (jnp.zeros_like(tail_state), jnp.zeros((), jnp.float32)),
    )
    before = doc_index(jnp.reshape(shard_index * rows_here - 1, (1,)), doc_ends)[0]
    incoming = incoming * (before == first_doc).astype(jnp.float32)
    queries = jax.nn.silu(query_sum).astype(jnp.bfloat16).reshape(rows_here, head_count, head_size)
    scores = jnp.einsum("thd,shd->hts", queries, key_rows, preferred_element_type=jnp.float32)
    causal = (
        (offsets[:, None] >= offsets[None, :]) & (doc_ids[:, None] == doc_ids[None, :])
    ).astype(jnp.float32)
    weights = (scores * causal[None]).astype(jnp.bfloat16)
    within = jnp.einsum("hts,she->the", weights, values, preferred_element_type=jnp.float32)
    carried = jnp.einsum(
        "thd,hde->the", queries, incoming.astype(jnp.bfloat16), preferred_element_type=jnp.float32
    )
    carried = carried * (doc_ids == first_doc).astype(jnp.float32)[:, None, None]
    mixed = within + carried
    sum_squares = lax.psum(jnp.sum(mixed * mixed, axis=(1, 2)), "fsdp")
    inverse_rms = lax.rsqrt(sum_squares / (head_count * lax.axis_size("fsdp") * head_size) + 1e-06)
    flat = mixed.reshape(rows_here, head_count * head_size)
    return (flat * inverse_rms[:, None] * norm_gain.astype(jnp.float32)[None, :]).astype(
        jnp.bfloat16
    )


def solution(mesh):
    return jax.shard_map(
        shards,
        mesh=mesh,
        in_specs=(P("seq", None), P("seq", "fsdp", None), P("seq", "fsdp", None), P(), P("fsdp")),
        out_specs=P("seq", "fsdp"),
        check_vma=False,
    )
```

profile of v0, /device:TPU:1, one launch (start us, length us, event | category | flops | bytes accessed | tf_op | source)
XLA Modules:
  0.0 427.5 jit_solution(9087954634818524678)
XLA Ops:
  9.6 1.2 compare_convert_fusion
  10.8 120.9 %all-gather.5.cloned.1.call-done = bf16[6144,4,256]{2,1,0:T(4,128)(2,1)} async-done(((bf16[192,4,256]{2,1,0:T(4,128)(2,1)}), bf16[6144,4,256]{2,1,0:T(4,128)(2,1)}) %all-gather.5.cloned.1.call-update) | async-done | bytes 12582928 | tf_op jit(solution)/shard_map/all_gather | solution.py:41
  131.7 9.3 %copy.33 = bf16[768,8,4,256]{3,1,2,0:T(8,128)(2,1)S(1)} copy(bf16[768,8,4,256]{3,2,1,0:T(4,128)(2,1)} %bitcast.40) | data formatting | bytes 25165824
  141.0 11.5 %multiply_convert_fusion.2 = bf16[768,1024]{1,0:T(8,128)(2,1)} fusion(bf16[768,6144]{1,0:T(8,128)(2,1)S(1)} %copy-done.2, bf16[6144,1024]{1,0:T(8,128)(2,1)S(1)} %bitcast.41), kind=kOutput, calls=%fused_computation.9 | convolution fusion | flops 9667608576 | bytes 23592960 | tf_op jit(solution)/shard_map/dot_general | solution.py:38
  152.5 2.9 reshape.105
  155.4 1.4 fusion.22
  156.9 1.9 copy.31
  158.7 1.3 fusion.13
  168.0 58.6 %all-reduce = f32[32]{0:T(128)S(1)} all-reduce(f32[32]{0:T(128)S(1)} %dynamic-update-slice), channel_id=1, replica_groups=mesh['seq'=32,'fsdp'=8] {'seq'}, use_global_device_ids=true, to_apply=%add | all-reduce | flops 32 | bytes 256
  226.9 11.6 %multiply_convert_fusion.4 = bf16[768,512]{0,1:T(8,128)(2,1)} fusion(bf16[768,6144]{1,0:T(8,128)(2,1)} %param.7, bf16[768,8,4,128]{3,2,1,0:T(4,128)(2,1)} %bitcast.47), kind=kOutput, calls=%fused_computation.17 | convolution fusion | flops 4833804288 | bytes 16515072 | tf_op jit(solution)/shard_map/dot_general | solution.py:38
  238.5 79.2 %all-gather.9.cloned.1.call-done = f32[128,128,128]{2,1,0:T(8,128)} async-done(((f32[4,128,128]{2,1,0:T(8,128)}), f32[128,128,128]{2,1,0:T(8,128)}) %all-gather.9.cloned.1.call-update) | async-done | bytes 8388624 | tf_op jit(solution)/shard_map/all_gather | solution.py:9
  317.7 78.4 %while.14 = (s32[]{:T(128)}, f32[4,128,128]{2,1,0:T(8,128)S(1)}, s32[]{:T(128)}, f32[32,4,128,128]{3,2,1,0:T(8,128)}, f32[32]{0:T(128)S(1)}, /*index=5*/s32[]{:T(128)}, f32[1]{0:T(128)}, s32[]{:T(128)}) while((s32[]{:T(128)}, f32[4,128,128]{2,1,0:T(8,128)S(1)}, s32[]{:T(128)}, f32[32,4,128,128]{3,2,1,0:T(8,128)}, f32[32]{0:T(128)S(1)}, ...), condition=%wide.region_3.4_spmd.clone, body=%wide.region_2.3_spmd.clone.sunk | while | flops 262149 | bytes 786569 | solution.py:18
  319.0 1.1 fusion.34
  321.6 1.1 fusion.34
  324.1 1.1 fusion.34
  326.6 1.1 fusion.34
  329.2 1.1 fusion.34
  331.7 1.1 fusion.34
  334.2 1.1 fusion.34
  336.7 1.1 fusion.34
  339.3 1.1 fusion.34
  341.8 1.1 fusion.34
  344.3 1.1 fusion.34
  346.9 1.1 fusion.34
  349.4 1.1 fusion.34
  351.9 1.1 fusion.34
  354.5 1.1 fusion.34
  357.0 1.1 fusion.34
  359.5 1.1 fusion.34
  362.0 1.1 fusion.34
  364.6 1.1 fusion.34
  367.1 1.1 fusion.34
  369.6 1.1 fusion.34
  372.2 1.1 fusion.34
  374.7 1.1 fusion.34
  377.2 1.1 fusion.34
  379.8 1.1 fusion.34
  382.3 1.1 fusion.34
  384.8 1.1 fusion.34
  387.3 1.1 fusion.34
  389.9 1.1 fusion.34
  392.4 1.1 fusion.34
  394.9 1.1 fusion.34
  396.1 2.7 fusion.19
  398.8 6.0 %fusion.10 = (f32[768]{0:T(1024)S(1)}, f32[4,128,768]{2,1,0:T(8,128)}) fusion(f32[4,128,768]{2,1,0:T(8,128)} %fusion.19, f32[768]{0:T(1024)S(1)} %get-tuple-element.130, bf16[768,4,128]{0,2,1:T(8,128)(2,1)S(1)} %copy.31, f32[768,768]{1,0:T(8,128)S(1)} %fusion.9, bf16[768,4,128]{0,2,1:T(8,128)(2,1)} %bitcast.44, bf16[768,4,128]{2,1,0:T(4,128)(2,1)} %copy-done), kind=kOutput, calls=%fused_computation.14 | convolution fusion | flops 1214250240 | bytes 7870464 | tf_op jit(solution)/shard_map/hts,she->the/dot_general | solution.py:74
  404.8 1.9 copy.25
  406.7 13.2 %psum.7 = f32[768]{0:T(1024)S(1)} all-reduce(f32[768]{0:T(1024)S(1)} %get-tuple-element.134), channel_id=1, replica_groups=mesh['seq'=32,'fsdp'=8] {'fsdp'}, use_global_device_ids=true, to_apply=%region_6.7 | all-reduce | flops 768 | bytes 6144 | tf_op jit(solution)/shard_map/psum | solution.py:80
  419.9 1.1 multiply_convert_fusion.3
  (62 shorter events, 27.3 us)
Async XLA Ops:
  6.5 125.1 %all-gather.5.cloned.1.call-start = ((), (), s32[]{:S(2)}) async-start(), calls=%async_computation | async-start | bytes 12976128 | tf_op jit(solution)/shard_map/all_gather | solution.py:41
  7.3 219.6 %all-gather.7.cloned.1.call-start = ((), (), s32[]{:S(2)}) async-start(), calls=%async_computation.1 | async-start | bytes 6488064 | tf_op jit(solution)/shard_map/all_gather | solution.py:40
  8.0 309.7 %all-gather.9.cloned.1.call-start = ((), (), s32[]{:S(2)}) async-start(), calls=%async_computation.2 | async-start | bytes 8650752 | tf_op jit(solution)/shard_map/all_gather | solution.py:9
  131.7 9.3 %copy-start.2 = (bf16[768,6144]{1,0:T(8,128)(2,1)S(1)}, bf16[768,6144]{1,0:T(8,128)(2,1)}, u32[]{:S(2)}) copy-start(bf16[768,6144]{1,0:T(8,128)(2,1)} %param.7) | copy-start | bytes 28311556
  156.9 11.1 %copy-start = (bf16[768,4,128]{2,1,0:T(4,128)(2,1)}, bf16[768,4,128]{2,1,0:T(4,128)(2,1)S(1)}, u32[]{:S(2)}) copy-start(bf16[768,4,128]{2,1,0:T(4,128)(2,1)S(1)} %get-tuple-element.128) | copy-start | bytes 2359300
  156.9 5.6 %copy-start.3 = (s32[8]{0:T(128)S(1)}, s32[8]{0:T(128)}, u32[]{:S(2)}) copy-start(s32[8]{0:T(128)} %param.10) | copy-start | bytes 100
  156.9 9.6 %copy-start.1 = (bf16[512]{0:T(512)(128)(2,1)S(1)}, bf16[512]{0:T(512)(128)(2,1)}, u32[]{:S(2)}) copy-start(bf16[512]{0:T(512)(128)(2,1)} %param.11) | copy-start | bytes 3076
  156.9 9.6 %copy-start.4 = (u32[256]{0:T(256)S(1)}, u32[256]{0:T(256)}, u32[]{:S(2)}) copy-start(u32[256]{0:T(256)} %constant.65) | copy-start | bytes 3076
Sparse Core Ops, SparseCore 0:
  9.9 121.7 all-gather.4
  134.3 85.5 all-gather.6
  222.5 95.1 all-gather.8
where the time goes:
time: 429 us; the launch traced here: 427 us
  waiting for transfers between devices  201 us (47%)
  blocking collectives  71.8 us (17%)
  local copies, waits for them, and re-layouts  41.2 us (10%)
  other arithmetic  39.8 us (9%)
  matrix products  33.1 us (8%)
  loops' own time  22.3 us (5%)
  between operations  17.7 us (4%)
    all_gather x1, waiting for transfers between devices, shards(): keyval_sum = project(lax.all_gather(w_keyval, 'seq', axis=0, tiled=True))  121 us
    all_gather x1, waiting for transfers between devices, carried_in(): pieces = jax.tree.map(lambda part: lax.all_gather(part, axis), value)  79.2 us
    unnamed x1, blocking collectives  58.6 us
    select_n x31, other arithmetic, step(): jnp.where(position < mine, new, old)  35.6 us
    dot_general x2, matrix products, project(): return jnp.dot(tokens, panel, preferred_element_type=jnp.float32)  23.1 us
    another operation x1, loops' own time, carried_in(): return lax.fori_loop(0, count - 1, step, running)  22.3 us
    dynamic_slice x31, local copies, waits for them, and re-layouts, step(): longer = join(running, jax.tree.map(lambda part: part[position], pieces))  20.6 us
    psum x1, blocking collectives, shards(): sum_squares = lax.psum(jnp.sum(mixed * mixed, axis=(1, 2)), 'fsdp')  13.2 us
  transfers between devices with their start and end apart: 3, of which 2 were waited for; matrix products, arithmetic and copies ran while one was open for 11% of the time, Pallas kernels for 0%

commit v1 on v0

--- a/solution.py
+++ b/solution.py
@@ -2,6 +2,11 @@
 import jax.numpy as jnp
 from jax import lax
 from jax.sharding import PartitionSpec as P
+
+
+def all_by_exchange(shard, name, dim):
+    stack = jnp.stack([shard] * lax.axis_size(name))
+    return jnp.concatenate(lax.all_to_all(stack, name, 0, 0), axis=dim)
 
 
 def carried_in(value, axis, join, neutral):
@@ -38,7 +43,7 @@
         return jnp.dot(tokens, panel, preferred_element_type=jnp.float32)
 
     query_sum = project(lax.all_gather(w_query, "seq", axis=0, tiled=True))
-    keyval_sum = project(lax.all_gather(w_keyval, "seq", axis=0, tiled=True))
+    keyval_sum = project(all_by_exchange(w_keyval, "seq", 0))
     keyval = (
         jax.nn.silu(keyval_sum).astype(jnp.bfloat16).reshape(rows_here, head_count, 2 * head_size)
     )

time: 429 us -> 587 us (1.37)
  waiting for transfers between devices: 201 us -> 331 us
  blocking collectives: 71.8 us -> 84.2 us
  starting transfers between devices: 0.08 us -> 12.2 us
    all_to_all x0 -> x1, waiting for transfers between devices: none -> 313 us  [all_by_exchange(): return jnp.concatenate(lax.all_to_all(stack, name, 0, 0), axis=dim)]
    all_gather x1 -> x0, waiting for transfers between devices: 121 us -> none  [shards(): keyval_sum = project(lax.all_gather(w_keyval, 'seq', axis=0, tiled=True))]
    all_gather x1, waiting for transfers between devices: 79.2 us -> 17.6 us  [carried_in(): pieces = jax.tree.map(lambda part: lax.all_gather(part, axis), value)]
    unnamed x1, blocking collectives: 58.6 us -> 71 us
    all_to_all x0 -> x1, starting transfers between devices: none -> 12.1 us  [all_by_exchange(): return jnp.concatenate(lax.all_to_all(stack, name, 0, 0), axis=dim)]
    another operation x0 -> x1, local copies, waits for them, and re-layouts: none -> 7.76 us  [all_by_exchange(): stack = jnp.stack([shard] * lax.axis_size(name))]
    unnamed x15 -> x13, local copies, waits for them, and re-layouts: 12.6 us -> 12.2 us
  transfers between devices with their start and end apart: 3 -> 3, of which waited for: 2 -> 2; matrix products, arithmetic and copies ran while one was open for 11% -> 8% of each run, Pallas kernels for 0% -> 0%
where the time goes in v1:
time: 587 us; the launch traced here: 585 us
  waiting for transfers between devices  331 us (56%)
  blocking collectives  84.2 us (14%)
  local copies, waits for them, and re-layouts  46.4 us (8%)
  other arithmetic  39.2 us (7%)
  matrix products  35.1 us (6%)
  loops' own time  18.6 us (3%)
  between operations  18.3 us (3%)
  starting transfers between devices  12.2 us (2%)
    all_to_all x1, waiting for transfers between devices, all_by_exchange(): return jnp.concatenate(lax.all_to_all(stack, name, 0, 0), axis=dim)  313 us
    unnamed x1, blocking collectives  71 us
    select_n x31, other arithmetic, step(): jnp.where(position < mine, new, old)  35.6 us
    dot_general x2, matrix products, project(): return jnp.dot(tokens, panel, preferred_element_type=jnp.float32)  25.1 us
    another operation x1, loops' own time, carried_in(): return lax.fori_loop(0, count - 1, step, running)  18.6 us
    dynamic_slice x31, local copies, waits for them, and re-layouts, step(): longer = join(running, jax.tree.map(lambda part: part[position], pieces))  18.3 us
    all_gather x1, waiting for transfers between devices, carried_in(): pieces = jax.tree.map(lambda part: lax.all_gather(part, axis), value)  17.6 us
    psum x1, blocking collectives, shards(): sum_squares = lax.psum(jnp.sum(mixed * mixed, axis=(1, 2)), 'fsdp')  13.2 us
  transfers between devices with their start and end apart: 3, of which 2 were waited for; matrix products, arithmetic and copies ran while one was open for 8% of the time, Pallas kernels for 0%

profile of v1, /device:TPU:1, one launch (start us, length us, event | category | flops | bytes accessed | tf_op | source)
XLA Modules:
  0.0 585.3 jit_solution(2083821556025856948)
XLA Ops:
  6.5 7.8 %stack.2 = bf16[32,192,4,256]{3,2,1,0:T(4,128)(2,1)} broadcast(bf16[192,4,256]{2,1,0:T(4,128)(2,1)} %param.9), dimensions={1,2,3} | broadcast | bytes 12976128 | tf_op jit(solution)/shard_map/stack | solution.py:8
  14.3 12.1 %all-to-all-start = ((bf16[32,192,4,256]{3,2,1,0:T(4,128)(2,1)}), bf16[32,192,4,256]{3,2,1,0:T(4,128)(2,1)}, u32[]{:S(2)}, u32[]{:S(2)}) async-start(bf16[32,192,4,256]{3,2,1,0:T(4,128)(2,1)} %stack.2), calls=%async_computation | async-start | bytes 25165824 | tf_op jit(solution)/shard_map/all_to_all | solution.py:9
  28.1 1.3 compare_convert_fusion
  29.5 313.1 %all-to-all-done = bf16[32,192,4,256]{3,2,1,0:T(4,128)(2,1)} async-done(((bf16[32,192,4,256]{3,2,1,0:T(4,128)(2,1)}), bf16[32,192,4,256]{3,2,1,0:T(4,128)(2,1)}, u32[]{:S(2)}, u32[]{:S(2)}) %all-to-all-start) | async-done | bytes 12582944 | tf_op jit(solution)/shard_map/all_to_all | solution.py:9
  342.6 8.9 %copy.33 = bf16[768,8,4,256]{3,1,2,0:T(8,128)(2,1)S(1)} copy(bf16[768,8,4,256]{3,2,1,0:T(4,128)(2,1)} %bitcast.16) | data formatting | bytes 25165824
  351.5 13.2 %multiply_convert_fusion.2 = bf16[768,1024]{1,0:T(8,128)(2,1)} fusion(bf16[768,6144]{1,0:T(8,128)(2,1)} %param.7, bf16[6144,1024]{1,0:T(8,128)(2,1)S(1)} %bitcast.41), kind=kOutput, calls=%fused_computation.9 | convolution fusion | flops 9667608576 | bytes 23592960 | tf_op jit(solution)/shard_map/dot_general | solution.py:43
  364.7 2.9 reshape.103
  367.6 1.4 fusion.22
  369.1 1.8 copy.31
  370.9 1.3 fusion.13
  380.4 71.0 %all-reduce = f32[32]{0:T(128)S(1)} all-reduce(f32[32]{0:T(128)S(1)} %dynamic-update-slice), channel_id=1, replica_groups=mesh['seq'=32,'fsdp'=8] {'seq'}, use_global_device_ids=true, to_apply=%add | all-reduce | flops 32 | bytes 256
  451.6 11.9 %multiply_convert_fusion.4 = bf16[768,512]{0,1:T(8,128)(2,1)} fusion(bf16[768,6144]{1,0:T(8,128)(2,1)} %param.7, bf16[768,8,4,128]{3,2,1,0:T(4,128)(2,1)} %bitcast.47), kind=kOutput, calls=%fused_computation.17 | convolution fusion | flops 4833804288 | bytes 16515072 | tf_op jit(solution)/shard_map/dot_general | solution.py:43
  463.5 17.6 %all-gather.6.cloned.1.call-done = f32[128,128,128]{2,1,0:T(8,128)} async-done(((f32[4,128,128]{2,1,0:T(8,128)}), f32[128,128,128]{2,1,0:T(8,128)}) %all-gather.6.cloned.1.call-update) | async-done | bytes 8388624 | tf_op jit(solution)/shard_map/all_gather | solution.py:14
  481.1 72.5 %while.14 = (s32[]{:T(128)}, f32[4,128,128]{2,1,0:T(8,128)S(1)}, s32[]{:T(128)}, f32[32,4,128,128]{3,2,1,0:T(8,128)}, f32[32]{0:T(128)S(1)}, /*index=5*/s32[]{:T(128)}, f32[1]{0:T(128)}, s32[]{:T(128)}) while((s32[]{:T(128)}, f32[4,128,128]{2,1,0:T(8,128)S(1)}, s32[]{:T(128)}, f32[32,4,128,128]{3,2,1,0:T(8,128)}, f32[32]{0:T(128)S(1)}, ...), condition=%wide.region_3.4_spmd.clone, body=%wide.region_2.3_spmd.clone.sunk | while | flops 262149 | bytes 786569 | solution.py:23
  482.3 1.1 fusion.34
  484.7 1.1 fusion.34
  487.0 1.1 fusion.34
  489.3 1.1 fusion.34
  491.7 1.1 fusion.34
  494.0 1.1 fusion.34
  496.4 1.1 fusion.34
  498.7 1.1 fusion.34
  501.0 1.1 fusion.34
  503.4 1.1 fusion.34
  505.7 1.1 fusion.34
  508.0 1.1 fusion.34
  510.4 1.1 fusion.34
  512.7 1.1 fusion.34
  515.1 1.1 fusion.34
  517.4 1.1 fusion.34
  519.7 1.1 fusion.34
  522.1 1.1 fusion.34
  524.4 1.1 fusion.34
  526.8 1.1 fusion.34
  529.1 1.1 fusion.34
  531.4 1.1 fusion.34
  533.8 1.1 fusion.34
  536.1 1.1 fusion.34
  538.5 1.1 fusion.34
  540.8 1.1 fusion.34
  543.1 1.1 fusion.34
  545.5 1.1 fusion.34
  547.8 1.1 fusion.34
  552.5 1.1 fusion.34
  553.6 2.7 fusion.19
  556.3 6.0 %fusion.10 = (f32[768]{0:T(1024)S(1)}, f32[4,128,768]{2,1,0:T(8,128)}) fusion(f32[4,128,768]{2,1,0:T(8,128)} %fusion.19, f32[768]{0:T(1024)S(1)} %get-tuple-element.130, bf16[768,4,128]{0,2,1:T(8,128)(2,1)S(1)} %copy.31, f32[768,768]{1,0:T(8,128)S(1)} %fusion.9, bf16[768,4,128]{0,2,1:T(8,128)(2,1)} %bitcast.44, bf16[768,4,128]{2,1,0:T(4,128)(2,1)} %copy-done), kind=kOutput, calls=%fused_computation.14 | convolution fusion | flops 1214250240 | bytes 7870464 | tf_op jit(solution)/shard_map/hts,she->the/dot_general | solution.py:79
  562.3 1.9 copy.25
  564.2 13.2 %psum.7 = f32[768]{0:T(1024)S(1)} all-reduce(f32[768]{0:T(1024)S(1)} %get-tuple-element.134), channel_id=1, replica_groups=mesh['seq'=32,'fsdp'=8] {'fsdp'}, use_global_device_ids=true, to_apply=%region_6.7 | all-reduce | flops 768 | bytes 6144 | tf_op jit(solution)/shard_map/psum | solution.py:85
  (60 shorter events, 26.0 us)
Async XLA Ops:
  14.3 12.9 %copy-start.2 = (s32[8]{0:T(128)S(1)}, s32[8]{0:T(128)}, u32[]{:S(2)}) copy-start(s32[8]{0:T(128)} %param.10) | copy-start | bytes 100
  14.3 328.3 %all-to-all-start = ((bf16[32,192,4,256]{3,2,1,0:T(4,128)(2,1)}), bf16[32,192,4,256]{3,2,1,0:T(4,128)(2,1)}, u32[]{:S(2)}, u32[]{:S(2)}) async-start(bf16[32,192,4,256]{3,2,1,0:T(4,128)(2,1)} %stack.2), calls=%async_computation | async-start | bytes 25165824 | tf_op jit(solution)/shard_map/all_to_all | solution.py:9
  26.4 425.2 %all-gather.4.cloned.1.call-start = ((), (), s32[]{:S(2)}) async-start(), calls=%async_computation.1 | async-start | bytes 6488064 | tf_op jit(solution)/shard_map/all_gather | solution.py:45
  27.1 454.0 %all-gather.6.cloned.1.call-start = ((), (), s32[]{:S(2)}) async-start(), calls=%async_computation.2 | async-start | bytes 8650752 | tf_op jit(solution)/shard_map/all_gather | solution.py:14
  369.1 11.3 %copy-start = (bf16[768,4,128]{2,1,0:T(4,128)(2,1)}, bf16[768,4,128]{2,1,0:T(4,128)(2,1)S(1)}, u32[]{:S(2)}) copy-start(bf16[768,4,128]{2,1,0:T(4,128)(2,1)S(1)} %get-tuple-element.128) | copy-start | bytes 2359300
  369.1 9.8 %copy-start.1 = (bf16[512]{0:T(512)(128)(2,1)S(1)}, bf16[512]{0:T(512)(128)(2,1)}, u32[]{:S(2)}) copy-start(bf16[512]{0:T(512)(128)(2,1)} %param.11) | copy-start | bytes 3076
  369.1 9.8 %copy-start.3 = (u32[256]{0:T(256)S(1)}, u32[256]{0:T(256)}, u32[]{:S(2)}) copy-start(u32[256]{0:T(256)} %constant.65) | copy-start | bytes 3076
Sparse Core Ops, SparseCore 0:
  29.8 203.0 all-gather.3
  372.3 108.7 all-gather.5
